TPU v7x, 128 devices: a whole 4x4x4 slice. The times are simulated.
128 devices in a mesh: grp: 8 (over y, core), tile: 16 (over z, x).
Axes of the slice: x: 4, y: 4, z: 4, core: 2. Of those that a mesh axis runs over, the one named last changes fastest.
Arguments:
- coefficient_array: bfloat16 [2097152, 256], P(('grp', 'tile')), may hold values from -6 to 6
- prior_thermal_field: bfloat16 [524288, 256], P(('grp', 'tile')), may hold values from -6 to 6
- gauge_cable_position: int32 [65536], P(('grp', 'tile')), may hold values from 0 to 4095
- gauge_damping_bucket: int32 [65536, 1], P(('grp', 'tile')), may hold values from 0 to 7; in each aligned block of 512 rows (0 to 511, 512 to 1023, ...) at most 128 rows name the same one
- gauge_misfit_sigma: float32 [65536], P(('grp', 'tile')), may hold values from 1 to 6
- jittered_observations: bfloat16 [65536, 256], P(('grp', 'tile')), may hold values from -12 to 12
Outputs:
- updated: bfloat16 [2097152, 256], P(('grp', 'tile'))
Inputs may be any that keep to these rules, and one draw needn't show every extreme that they name: `gauge_damping_bucket`: of the sensors of one device, at most 128 belong to one group.
All inputs are finite; a program needn't handle non-finite values.
Results may differ from a plain program's by a relative error of at most 0.0093.
Values may be sent and summed in bfloat16 or wider, within the bound.
A program may use at most 64 MiB of HBM per device.

v0:
```python
import math

import jax
import jax.numpy as jnp
from jax import lax
from jax.sharding import PartitionSpec as P


def solve_group(gram, cross):
    factor = jnp.linalg.cholesky(gram + jnp.eye(gram.shape[0], dtype=jnp.float32))
    return jax.scipy.linalg.cho_solve((factor, True), cross)


def shards(
    coefficient_array,
    prior_thermal_field,
    gauge_cable_position,
    gauge_damping_bucket,
    gauge_misfit_sigma,
    jittered_observations,
):
    members = coefficient_array.shape[1]
    root_scale = math.sqrt(members - 1)
    groups = lax.axis_size("grp")
    sensors = gauge_cable_position.shape[0]
    capacity = sensors // 4
    kept_indices = jnp.take(prior_thermal_field, gauge_cable_position, axis=0).astype(jnp.float32)
    member_mean = jnp.mean(kept_indices, axis=1, keepdims=True)
    scaled = ((kept_indices - member_mean) / (gauge_misfit_sigma[:, None] * root_scale)).astype(
        jnp.bfloat16
    )
    misfit = (
        (jittered_observations.astype(jnp.float32) - kept_indices) / gauge_misfit_sigma[:, None]
    ).astype(jnp.bfloat16)
    group_ids = gauge_damping_bucket[:, 0]
    one_hot = (group_ids[:, None] == jnp.arange(groups, dtype=jnp.int32)[None, :]).astype(jnp.int32)
    slot_index = jnp.sum((jnp.cumsum(one_hot, axis=0) - 1) * one_hot, axis=1)
    target = group_ids * capacity + slot_index
    send_scaled = jnp.zeros((groups * capacity, members), jnp.bfloat16).at[target].set(scaled)
    send_misfit = jnp.zeros((groups * capacity, members), jnp.bfloat16).at[target].set(misfit)
    send_scaled = send_scaled.reshape(groups, capacity, members)
    send_misfit = send_misfit.reshape(groups, capacity, members)
    got_scaled, got_misfit = (
        lax.all_to_all(send_scaled, "grp", split_axis=0, concat_axis=0, tiled=True),
        lax.all_to_all(send_misfit, "grp", split_axis=0, concat_axis=0, tiled=True),
    )
    flat_scaled = got_scaled.reshape(-1, members)
    flat_misfit = got_misfit.reshape(-1, members)
    gram = jnp.einsum("rn,rm->nm", flat_scaled, flat_scaled, preferred_element_type=jnp.float32)
    cross = jnp.einsum("rn,rm->nm", flat_scaled, flat_misfit, preferred_element_type=jnp.float32)
    gram_total, cross_total = lax.psum((gram, cross), "tile")
    transform = (solve_group(gram_total, cross_total) / root_scale).astype(jnp.bfloat16)
    values = coefficient_array.astype(jnp.float32)
    anomaly = (values - jnp.mean(values, axis=1, keepdims=True)).astype(jnp.bfloat16)
    change = jnp.dot(anomaly, transform, preferred_element_type=jnp.float32)
    return (values + change).astype(jnp.bfloat16)


def solution(mesh):
    placed = (
        P(("grp", "tile"), None),
        P(("grp", "tile"), None),
        P(("grp", "tile")),
        P(("grp", "tile"), None),
        P(("grp", "tile")),
        P(("grp", "tile"), None),
    )
    return jax.shard_map(
        shards, mesh=mesh, in_specs=placed, out_specs=P(("grp", "tile"), None), check_vma=False
    )
```

profile of v0, /device:TPU:0, one launch (start us, length us, event | category | flops | bytes accessed | tf_op | source)
XLA Modules:
  0.0 217.8 jit_solution(14541110766488756284)
XLA Ops:
  6.5 0.0 copy-start
  6.5 0.8 compare_and_fusion
  7.4 0.7 compare_select_fusion.1
  8.1 0.7 fusion.32
  8.8 1.1 reduce-window.6
  9.9 0.2 slice_reduce_fusion
  10.1 0.8 fusion.31
  10.9 0.7 compare_select_fusion
  11.6 0.0 copy-done
  11.6 1.9 gather_fusion
  13.6 0.2 convert_reduce_fusion.1
  13.8 0.7 broadcast_multiply_fusion.1
  14.5 3.4 %scatter_custom_fusion = bf16[1024,256]{1,0:T(8,128)(2,1)} fusion(s32[512]{0:T(512)S(1)} %bitcast.61, f32[512]{0:T(512)S(1)} %get-tuple-element.31, f32[512]{0:T(512)S(1)} %get-tuple-element.32, bf16[]{:T(256)} %constant.116.clone.1, bf16[512,256]{1,0:T(8,128)(2,1)S(1)} %gather_fusion, pred[512]{0:T(512)(128)(4,1)S(1)} %compare_and_fusion), kind=kCustom, calls=%fused_computation.24 | custom fusion | flops 655360 | bytes 791042 | tf_op jit(solution)/shard_map/scatter | solution.py:39
  17.9 4.6 %all-to-all-start = ((bf16[8,128,256]{2,1,0:T(8,128)(2,1)}), bf16[8,128,256]{2,1,0:T(8,128)(2,1)S(1)}, u32[]{:S(2)}, u32[]{:S(2)}) async-start(bf16[8,128,256]{2,1,0:T(8,128)(2,1)} %bitcast.6), calls=%async_computation | async-start | bytes 1048576 | tf_op jit(solution)/shard_map/all_to_all | solution.py:44
  22.4 3.7 %scatter_custom_fusion.1 = bf16[1024,256]{1,0:T(8,128)(2,1)} fusion(s32[512]{0:T(512)S(1)} %bitcast.62, bf16[512,256]{1,0:T(8,128)(2,1)} %param.11, f32[512]{0:T(512)} %param.10, bf16[]{:T(256)} %constant.116.clone.1, bf16[512,256]{1,0:T(8,128)(2,1)S(1)} %gather_fusion, pred[512]{0:T(512)(128)(4,1)S(1)} %compare_and_fusion), kind=kCustom, calls=%fused_computation.25 | custom fusion | flops 786432 | bytes 1051138 | tf_op jit(solution)/shard_map/scatter | solution.py:40
  26.1 6.6 %all-to-all-done = bf16[8,128,256]{2,1,0:T(8,128)(2,1)S(1)} async-done(((bf16[8,128,256]{2,1,0:T(8,128)(2,1)}), bf16[8,128,256]{2,1,0:T(8,128)(2,1)S(1)}, u32[]{:S(2)}, u32[]{:S(2)}) %all-to-all-start) | async-done | bytes 524320 | tf_op jit(solution)/shard_map/all_to_all | solution.py:44
  32.8 3.5 %all-to-all-start.1 = ((bf16[8,128,256]{2,1,0:T(8,128)(2,1)}), bf16[8,128,256]{2,1,0:T(8,128)(2,1)S(1)}, u32[]{:S(2)}, u32[]{:S(2)}) async-start(bf16[8,128,256]{2,1,0:T(8,128)(2,1)} %bitcast.12), calls=%async_computation.1 | async-start | bytes 1048576 | tf_op jit(solution)/shard_map/all_to_all | solution.py:45
  36.3 0.2 all-reduce.4.cloned.1.call-start
  36.5 5.2 %convert_reduce_fusion = f32[16384]{0:T(1024)S(1)} fusion(bf16[16384,256]{1,0:T(8,128)(2,1)} %param.6), kind=kLoop, calls=%fused_computation.7 | loop fusion | flops 8372224 | bytes 8454144 | tf_op jit(solution)/shard_map/reduce_sum | solution.py:54
  41.7 1.0 convolution_bitcast_fusion.1
  42.8 3.7 %all-to-all-done.1 = bf16[8,128,256]{2,1,0:T(8,128)(2,1)S(1)} async-done(((bf16[8,128,256]{2,1,0:T(8,128)(2,1)}), bf16[8,128,256]{2,1,0:T(8,128)(2,1)S(1)}, u32[]{:S(2)}, u32[]{:S(2)}) %all-to-all-start.1) | async-done | bytes 524320 | tf_op jit(solution)/shard_map/all_to_all | solution.py:45
  46.5 1.0 convolution_bitcast_fusion
  47.5 0.0 all-reduce.4.cloned.1.call-update
  47.6 86.4 %all-reduce.4.cloned.1.call-done = (f32[256,256]{1,0:T(8,128)}, f32[256,256]{0,1:T(8,128)}) async-done(((f32[256,256]{1,0:T(8,128)}, f32[256,256]{0,1:T(8,128)}), (f32[256,256]{1,0:T(8,128)}, f32[256,256]{0,1:T(8,128)})) %all-reduce.4.cloned.1.call-update) | async-done | bytes 524304 | tf_op jit(solution)/shard_map/psum | solution.py:51
  133.9 1.0 convert_add_fusion.1
  134.9 0.1 copy.13
  135.0 1.0 fusion.13
  136.1 11.7 %cholesky.50 = f32[128,128]{1,0:T(8,128)S(1)} custom-call(f32[128,128]{1,0:T(8,128)S(1)} %cholesky.118), custom_call_target="Cholesky" | custom-call | tf_op jit(solution)/shard_map/jit(cholesky)/cholesky | solution.py:10
  147.8 0.6 compare_reduce_fusion.1
  148.4 9.8 %custom-call.18 = f32[1,128,128]{1,2,0:T(8,128)S(1)} custom-call(f32[1,128,128]{2,1,0:T(8,128)S(1)} %get-tuple-element.28), custom_call_target="InvertDiagBlocksLowerTriangular" | custom-call | tf_op jit(solution)/shard_map/jit(cholesky)/cholesky | solution.py:10
  158.3 0.2 constant_dynamic-update-slice_fusion.1
  158.5 0.3 convolution_subtract_fusion.2
  158.8 11.7 %cholesky.105 = f32[128,128]{1,0:T(8,128)S(1)} custom-call(f32[128,128]{1,0:T(8,128)S(1)} %convolution_subtract_fusion.2), custom_call_target="Cholesky" | custom-call | tf_op jit(solution)/shard_map/jit(cholesky)/cholesky | solution.py:10
  170.5 0.7 compare_reduce_fusion
  172.5 0.1 triangular_solve.69
  172.6 3.9 %while.1 = (s32[]{:T(128)}, f32[256,256]{1,0:T(8,128)S(1)}, s32[2,2]{1,0:T(2,128)S(1)}, f32[2,128,128]{2,1,0:T(8,128)S(1)}, s32[]{:T(128)}) while((s32[]{:T(128)}, f32[256,256]{1,0:T(8,128)S(1)}, s32[2,2]{1,0:T(2,128)S(1)}, f32[2,128,128]{2,1,0:T(8,128)S(1)}, s32[]{:T(128)}) %tuple.23), condition=%wide.while_cond, body=%wide.while_body.sunk | while | flops 2 | bytes 131189 | solution.py:11
  172.6 0.6 fusion.48
  173.2 1.4 bitcast_dynamic-update-slice_fusion.2
  174.6 0.6 fusion.48
  175.2 1.4 bitcast_dynamic-update-slice_fusion.2
  176.5 19.9 %custom-call.19 = f32[2,128,128]{1,2,0:T(8,128)S(1)} custom-call(f32[2,128,128]{2,1,0:T(8,128)S(1)} %get-tuple-element.12), custom_call_target="InvertDiagBlocksLowerTriangular" | custom-call | tf_op jit(solution)/shard_map/jit(_cho_solve)/triangular_solve | solution.py:11
  196.4 1.2 fusion.20
  197.7 1.2 convolution_subtract_fusion.1
  198.8 0.3 fusion.28
  199.1 0.3 fusion.27
  199.4 0.3 convolution_subtract_fusion
  199.7 0.3 fusion.26
  200.0 10.9 %fusion = bf16[16384,256]{1,0:T(8,128)(2,1)} fusion(bf16[16384,256]{1,0:T(8,128)(2,1)} %param.6, f32[16384]{0:T(1024)S(1)} %broadcast_multiply_fusion, f32[128,256]{1,0:T(8,128)S(1)} %fusion.27, f32[128,256]{1,0:T(8,128)S(1)} %fusion.26), kind=kOutput, calls=%fused_computation.8 | convolution fusion | flops 2172846080 | bytes 17104896 | tf_op jit(solution)/shard_map/dot_general | solution.py:55
  (13 shorter events, 0.2 us)
Async XLA Ops:
  6.5 5.1 %copy-start = (bf16[4096,256]{1,0:T(8,128)(2,1)S(1)}, bf16[4096,256]{1,0:T(8,128)(2,1)}, u32[]{:S(2)}) copy-start(bf16[4096,256]{1,0:T(8,128)(2,1)} %param.7) | copy-start | bytes 6291460
  17.9 14.9 %all-to-all-start = ((bf16[8,128,256]{2,1,0:T(8,128)(2,1)}), bf16[8,128,256]{2,1,0:T(8,128)(2,1)S(1)}, u32[]{:S(2)}, u32[]{:S(2)}) async-start(bf16[8,128,256]{2,1,0:T(8,128)(2,1)} %bitcast.6), calls=%async_computation | async-start | bytes 1048576 | tf_op jit(solution)/shard_map/all_to_all | solution.py:44
  32.8 13.7 %all-to-all-start.1 = ((bf16[8,128,256]{2,1,0:T(8,128)(2,1)}), bf16[8,128,256]{2,1,0:T(8,128)(2,1)S(1)}, u32[]{:S(2)}, u32[]{:S(2)}) async-start(bf16[8,128,256]{2,1,0:T(8,128)(2,1)} %bitcast.12), calls=%async_computation.1 | async-start | bytes 1048576 | tf_op jit(solution)/shard_map/all_to_all | solution.py:45
  36.3 97.7 %all-reduce.4.cloned.1.call-start = ((), (), s32[]{:S(2)}) async-start(), calls=%async_computation.2 | async-start | bytes 1048576 | tf_op jit(solution)/shard_map/psum | solution.py:51
Sparse Core Ops, SparseCore 0:
  47.7 86.2 all-reduce.3
where the time goes:
time: 218 us
  waiting for transfers between devices  96.7 us (44%)
  other arithmetic  74.6 us (34%)
  matrix products  17 us (8%)
  between operations  14.8 us (7%)
  starting transfers between devices  8.3 us (4%)
  local copies, waits for them, and re-layouts  6.3 us (3%)
    psum x1, waiting for transfers between devices, shards(): gram_total, cross_total = lax.psum((gram, cross), 'tile')  86.4 us
    another operation x7, other arithmetic, solve_group(): jnp.linalg.cholesky(gram + jnp.eye(gram.shape[0], dtype=jnp.float32))  34.6 us
    another operation x3, other arithmetic, solve_group(): return jax.scipy.linalg.cho_solve((factor, True), cross)  19.9 us
    dot_general x1, matrix products, shards(): change = jnp.dot(anomaly, transform, preferred_element_type=jnp.float32)  10.9 us
    all_to_all x1, waiting for transfers between devices, shards(): lax.all_to_all(send_scaled, 'grp', split_axis=0, concat_axis=0, tiled=True)  6.62 us
    reduce_sum x1, other arithmetic, shards(): jnp.mean(values, axis=1, keepdims=True)  5.22 us
    all_to_all x1, starting transfers between devices, shards(): lax.all_to_all(send_scaled, 'grp', split_axis=0, concat_axis=0, tiled=True)  4.58 us
  transfers between devices with their start and end apart: 3, of which 3 were waited for; matrix products, arithmetic and copies ran while one was open for 5% of the time, Pallas kernels for 0%

commit v1 on v0

v1 whole, which is shorter than its diff:
```python
import functools
import math

import jax
import jax.numpy as jnp
from jax import lax
from jax.experimental import pallas as pl
from jax.experimental.pallas import tpu as pltpu
from jax.sharding import PartitionSpec as P

F32, BF16 = jnp.float32, jnp.bfloat16
MESH = pl.DeviceIdType.MESH
VMEM = pl.BlockSpec(memory_space=pltpu.VMEM)
ANY = pl.BlockSpec(memory_space=pl.ANY)
BLOCK = 512
SAFE_BOUND = 256.0
ROW_TILE = 2048


def dot(a, b):
    return lax.dot_general(a, b, (((1,), (0,)), ((), ())), preferred_element_type=F32)


def dot_rows(a, b):
    return lax.dot_general(a, b, (((0,), (0,)), ((), ())), preferred_element_type=F32)


def split(a):
    high = a.astype(BF16)
    return high, (a - high.astype(F32)).astype(BF16)


def dot_split(a, b_high, b_low):
    a_high, a_low = split(a)
    return dot(a_high, b_high) + (dot(a_low, b_high) + dot(a_high, b_low))


def exchange(
    groups,
    tiles,
    position,
    bucket,
    sigma,
    field,
    observed,
    gram_out,
    cross_out,
    field_vmem,
    picked,
    send_scaled,
    send_misfit,
    got_scaled,
    got_misfit,
    part,
    pieces,
    mine,
    field_sem,
    send_sem,
    got_sem,
    piece_send,
    piece_got,
    whole_send,
    whole_got,
):
    cells, members = field.shape
    sensors = position.shape[1]
    capacity = send_scaled.shape[1]
    rows = members // tiles
    root_scale = math.sqrt(members - 1)
    my_group, my_tile = lax.axis_index("grp"), lax.axis_index("tile")

    def other_group(offset):
        return lax.rem(my_group + offset, groups)

    def other_tile(offset):
        return lax.rem(my_tile + offset, tiles)

    loads = []
    for block in range(cells // BLOCK):
        part_rows = pl.ds(block * BLOCK, BLOCK)
        loads.append(
            pltpu.make_async_copy(field.at[part_rows], field_vmem.at[part_rows], field_sem.at[block])
        )
        loads[-1].start()

    barrier = pltpu.get_barrier_semaphore()
    for offset in range(1, groups):
        pl.semaphore_signal(
            barrier, inc=1, device_id={"grp": other_group(offset)}, device_id_type=MESH
        )
    for offset in range(1, tiles):
        pl.semaphore_signal(
            barrier, inc=1, device_id={"tile": other_tile(offset)}, device_id_type=MESH
        )

    cell = position[...]
    group = bucket[...]
    facts = jnp.concatenate(
        [cell.astype(F32), sigma[...], jnp.zeros((6, sensors), F32)], axis=0
    ).T
    cell_column, sigma_column = facts[:, 0:1].astype(jnp.int32), facts[:, 1:2]

    lane = lax.broadcasted_iota(jnp.int32, (sensors, sensors), 1)
    row = lax.broadcasted_iota(jnp.int32, (sensors, sensors), 0)
    earlier = (row < lane).astype(F32).astype(BF16)
    member_of = (lax.broadcasted_iota(jnp.int32, (groups, sensors), 0) == group).astype(F32)
    before = dot(member_of.astype(BF16), earlier)
    rank = jnp.sum(before * member_of, axis=0, keepdims=True).astype(jnp.int32)
    target = group * capacity + rank

    for block in range(cells // BLOCK):
        part_rows = pl.ds(block * BLOCK, BLOCK)
        chosen = (
            lax.broadcasted_iota(jnp.int32, (sensors, BLOCK), 1) == cell_column - block * BLOCK
        )
        loads[block].wait()
        value = dot(chosen.astype(F32).astype(BF16), field_vmem[part_rows, :])
        if block == 0:
            picked[...] = value
        else:
            picked[...] += value

    kept = picked[...]
    mean = jnp.mean(kept, axis=1, keepdims=True)
    scaled = ((kept - mean) / (sigma_column * root_scale)).astype(BF16)
    misfit = ((observed[...].astype(F32) - kept) / sigma_column).astype(BF16)

    def place(values, offset):
        slot = other_group(offset) * capacity + lax.broadcasted_iota(
            jnp.int32, (capacity, sensors), 0
        )
        return dot((slot == target).astype(F32).astype(BF16), values).astype(BF16)

    def row_copy(source, landing, kind, offset):
        return pltpu.make_async_remote_copy(
            src_ref=source.at[offset],
            dst_ref=landing.at[offset],
            send_sem=send_sem.at[kind, offset],
            recv_sem=got_sem.at[kind, offset],
            device_id={"grp": other_group(offset)},
            device_id_type=MESH,
        )

    order = [4, 3, 5, 2, 6, 1, 7, 0]
    sends = []
    for kind, (values, buffer, landing) in enumerate(
        ((scaled, send_scaled, got_scaled), (misfit, send_misfit, got_misfit))
    ):
        ready = None
        for offset in order:
            buffer[offset] = place(values, offset)
            if kind == 0 and ready is None:
                pl.semaphore_wait(barrier, groups + tiles - 2)
            if ready is not None:
                ready.start()
                sends.append(ready)
            ready = row_copy(buffer, landing, kind, offset) if offset else None

    def piece_copy(which, offset):
        target_rows = pl.ds(pl.multiple_of(other_tile(offset) * rows, rows), rows)
        return pltpu.make_async_remote_copy(
            src_ref=part.at[which, target_rows],
            dst_ref=pieces.at[which, offset],
            send_sem=piece_send.at[which, offset],
            recv_sem=piece_got.at[which, offset],
            device_id={"tile": other_tile(offset)},
            device_id_type=MESH,
        )

    my_rows = pl.ds(pl.multiple_of(my_tile * rows, rows), rows)

    def whole_copy(which, out, offset):
        return pltpu.make_async_remote_copy(
            src_ref=mine.at[which],
            dst_ref=out.at[my_rows],
            send_sem=whole_send.at[which, offset],
            recv_sem=whole_got.at[which, offset],
            device_id={"tile": other_tile(offset)},
            device_id_type=MESH,
        )

    def whole_wait(which, out, offset):
        source = lax.rem(my_tile + tiles - offset, tiles)
        source_rows = pl.ds(pl.multiple_of(source * rows, rows), rows)
        pltpu.make_async_remote_copy(
            src_ref=mine.at[which],
            dst_ref=out.at[source_rows],
            send_sem=whole_send.at[which, offset],
            recv_sem=whole_got.at[which, offset],
            device_id={"tile": other_tile(offset)},
            device_id_type=MESH,
        ).wait_recv()

    def add_up(which, right_own, right_got):
        part[which] = dot_rows(send_scaled[0], right_own[0])
        for offset in order[:-1]:
            row_copy(send_scaled, got_scaled, which, offset).wait_recv()
            part[which] += dot_rows(got_scaled[offset], right_got[offset])
        for offset in range(1, tiles):
            piece_copy(which, offset).start()

    def spread(which, out):
        total = part[which, my_rows]
        for offset in range(1, tiles):
            piece_copy(which, offset).wait_recv()
            total = total + pieces[which, offset]
        mine[which] = total
        out[my_rows] = total
        for offset in range(1, tiles):
            whole_copy(which, out, offset).start()

    add_up(0, send_scaled, got_scaled)
    spread(0, gram_out)
    add_up(1, send_misfit, got_misfit)
    spread(1, cross_out)
    for which, out in ((0, gram_out), (1, cross_out)):
        for offset in range(1, tiles):
            whole_wait(which, out, offset)
    for copy in sends:
        copy.wait_send()
    for which, out in ((0, gram_out), (1, cross_out)):
        for offset in range(1, tiles):
            piece_copy(which, offset).wait_send()
            whole_copy(which, out, offset).wait_send()


def sums(groups, tiles, position, bucket, sigma, field, observed):
    cells, members = field.shape
    sensors = position.shape[1]
    capacity = sensors // 4
    rows = members // tiles
    return pl.pallas_call(
        functools.partial(exchange, groups, tiles),
        out_shape=[jax.ShapeDtypeStruct((members, members), F32)] * 2,
        in_specs=[VMEM, VMEM, VMEM, ANY, VMEM],
        out_specs=[VMEM, VMEM],
        scratch_shapes=[
            pltpu.VMEM((cells, members), BF16),
            pltpu.VMEM((sensors, members), F32),
            pltpu.VMEM((groups, capacity, members), BF16),
            pltpu.VMEM((groups, capacity, members), BF16),
            pltpu.VMEM((groups, capacity, members), BF16),
            pltpu.VMEM((groups, capacity, members), BF16),
            pltpu.VMEM((2, members, members), F32),
            pltpu.VMEM((2, tiles, rows, members), F32),
            pltpu.VMEM((2, rows, members), F32),
            pltpu.SemaphoreType.DMA((cells // BLOCK,)),
            pltpu.SemaphoreType.DMA((2, groups)),
            pltpu.SemaphoreType.DMA((2, groups)),
            pltpu.SemaphoreType.DMA((2, tiles)),
            pltpu.SemaphoreType.DMA((2, tiles)),
            pltpu.SemaphoreType.DMA((2, tiles)),
            pltpu.SemaphoreType.DMA((2, tiles)),
        ],
        compiler_params=pltpu.CompilerParams(
            collective_id=0, has_side_effects=True, vmem_limit_bytes=24 << 20
        ),
        name="sums",
    )(position, bucket, sigma, field, observed)


def apply(gram, cross, values, out, loaded, stored, inverse, power, transform, load_sem, store_sem):
    total_rows, members = values.shape
    steps = total_rows // ROW_TILE

    def load(step):
        part = pl.ds(step * ROW_TILE, ROW_TILE)
        return pltpu.make_async_copy(values.at[part], loaded.at[part], load_sem.at[step])

    for step in range(steps):
        load(step).start()

    identity = (
        lax.broadcasted_iota(jnp.int32, (members, members), 0)
        == lax.broadcasted_iota(jnp.int32, (members, members), 1)
    ).astype(F32)
    matrix = gram[...] + identity
    bound = jnp.max(jnp.sum(jnp.abs(matrix), axis=1, keepdims=True))

    @pl.when(bound <= SAFE_BOUND)
    def _():
        scale = 1.0 / bound
        power[...] = identity - matrix * scale
        inverse[...] = identity * scale

        def double(_, reach):
            high, low = split(power[...])
            now = inverse[...]
            inverse[...] = now + dot_split(now, high, low)
            power[...] = dot(high, high) + (dot(high, low) + dot(low, high))
            return reach * 2.0

        lax.while_loop(lambda reach: reach < bound * 14.0, lambda reach: double(0, reach), 1.0)
        now = inverse[...]
        high, low = split(now)
        rest = identity - dot_split(gram[...] + identity, high, low)
        rest_high, rest_low = split(rest)
        inverse[...] = now + dot_split(now, rest_high, rest_low)

    @pl.when(bound > SAFE_BOUND)
    def _():
        inverse[...] = matrix
        line = lax.broadcasted_iota(jnp.int32, (members, 1), 0)
        spot = lax.broadcasted_iota(jnp.int32, (1, members), 1)

        def eliminate(step, _):
            now = inverse[...]
            here, there = (line == step), (spot == step)
            row = jnp.sum(jnp.where(here, now, 0.0), axis=0, keepdims=True)
            column = jnp.sum(jnp.where(there, now, 0.0), axis=1, keepdims=True)
            pivot = jnp.sum(jnp.where(there, row, 0.0), axis=1, keepdims=True)
            row = jnp.where(there, 1.0, row) / pivot
            column = jnp.where(here, 0.0, column)
            base = jnp.where(there, 0.0, now)
            inverse[...] = jnp.where(here, row, base - column * row)
            return 0

        lax.fori_loop(0, members, eliminate, 0)

    high, low = split(cross[...])
    weights = dot_split(inverse[...], high, low)
    transform[...] = (weights / math.sqrt(members - 1)).astype(BF16)

    def store(step, slot):
        part = pl.ds(step * ROW_TILE, ROW_TILE)
        return pltpu.make_async_copy(stored.at[slot], out.at[part], store_sem.at[slot])

    for step in range(steps):
        slot = step % 2
        load(step).wait()
        now = loaded[pl.ds(step * ROW_TILE, ROW_TILE), :].astype(F32)
        anomaly = (now - jnp.mean(now, axis=1, keepdims=True)).astype(BF16)
        change = dot(anomaly, transform[...])
        if step >= 2:
            store(step - 2, slot).wait()
        stored[slot] = (now + change).astype(BF16)
        store(step, slot).start()
    for step in range(steps - 2, steps):
        store(step, step % 2).wait()


def update(gram, cross, values):
    total_rows, members = values.shape
    steps = total_rows // ROW_TILE
    return pl.pallas_call(
        apply,
        out_shape=jax.ShapeDtypeStruct(values.shape, values.dtype),
        in_specs=[VMEM, VMEM, ANY],
        out_specs=ANY,
        scratch_shapes=[
            pltpu.VMEM((total_rows, members), BF16),
            pltpu.VMEM((2, ROW_TILE, members), BF16),
            pltpu.VMEM((members, members), F32),
            pltpu.VMEM((members, members), F32),
            pltpu.VMEM((members, members), BF16),
            pltpu.SemaphoreType.DMA((steps,)),
            pltpu.SemaphoreType.DMA((2,)),
        ],
        compiler_params=pltpu.CompilerParams(vmem_limit_bytes=48 << 20),
        name="update",
    )(gram, cross, values)


def solution(mesh):
    groups, tiles = mesh.shape["grp"], mesh.shape["tile"]

    def shards(coefficients, field, position, bucket, sigma, observed):
        sensors = position.shape[0]
        gram, cross = sums(
            groups,
            tiles,
            position.reshape(1, sensors),
            bucket.reshape(1, sensors),
            sigma.reshape(1, sensors),
            field,
            observed,
        )
        return update(gram, cross, coefficients)

    rows, flat = P(("grp", "tile"), None), P(("grp", "tile"))
    return jax.shard_map(
        shards,
        mesh=mesh,
        in_specs=(rows, rows, flat, rows, flat, rows),
        out_specs=rows,
        check_vma=False,
    )
```

time: 218 us -> 58.6 us (0.27)
  waiting for transfers between devices: 96.7 us -> 0 us
  other arithmetic: 74.6 us -> 0 us
  Pallas kernels: 0 us -> 53.6 us
  matrix products: 17 us -> 0 us
  between operations: 14.8 us -> 0.17 us
  starting transfers between devices: 8.3 us -> 0 us
    psum x1 -> x0, waiting for transfers between devices: 86.4 us -> none  [shards(): gram_total, cross_total = lax.psum((gram, cross), 'tile')]
    another operation x12 -> x0, other arithmetic: 55.7 us -> none  [the longest x7 34.6 us: solve_group(): jnp.linalg.cholesky(gram + jnp.eye(gram.shape[0], dtype=jnp.float32))]
    pallas_call x0 -> x2, Pallas kernels: none -> 53.6 us  [the longest x1 40 us: sums(): pl.pallas_call(functools.partial(exchange, groups, tiles), out_shape=[jax...]
    dot_general x3 -> x0, matrix products: 13 us -> none  [the longest x1 10.9 us: shards(): change = jnp.dot(anomaly, transform, preferred_element_type=jnp.float32)]
    all_to_all x2 -> x0, waiting for transfers between devices: 10.4 us -> none  [the longest x1 6.62 us: shards(): lax.all_to_all(send_scaled, 'grp', split_axis=0, concat_axis=0, tiled=True)]
    all_to_all x2 -> x0, starting transfers between devices: 8.07 us -> none  [the longest x1 4.58 us: shards(): lax.all_to_all(send_scaled, 'grp', split_axis=0, concat_axis=0, tiled=True)]
    scatter x2 -> x0, other arithmetic: 7.07 us -> none  [the longest x1 3.7 us: shards(): jnp.zeros((groups * capacity, members), jnp.bfloat16).at[target].set(misfit)]
    reduce_sum x3 -> x0, other arithmetic: 6.23 us -> none  [the longest x1 5.22 us: shards(): jnp.mean(values, axis=1, keepdims=True)]
  transfers between devices with their start and end apart: 3 -> 0, of which waited for: 3 -> 0; matrix products, arithmetic and copies ran while one was open for 5% -> 0% of each run, Pallas kernels for 0% -> 0%
where the time goes in v1:
time: 58.6 us; the launch traced here: 58.4 us
  Pallas kernels  53.6 us (91%)
  local copies, waits for them, and re-layouts  4.58 us (8%)
    pallas_call x1, Pallas kernels, sums(): pl.pallas_call(functools.partial(exchange, groups, tiles), out_shape=[jax...  40 us
    pallas_call x1, Pallas kernels, update(): pl.pallas_call(apply, out_shape=jax.ShapeDtypeStruct(values.shape, values...  13.7 us
    unnamed x10, local copies, waits for them, and re-layouts  4.58 us

profile of v1, /device:TPU:0, one launch (start us, length us, event | category | flops | bytes accessed | tf_op | source)
XLA Modules:
  0.0 58.4 jit_solution(18147602300901756423)
XLA Ops:
  0.0 0.0 copy-start
  0.0 1.6 %copy-done = bf16[4096,256]{1,0:T(8,128)(2,1)S(1)} copy-done((bf16[4096,256]{1,0:T(8,128)(2,1)S(1)}, bf16[4096,256]{1,0:T(8,128)(2,1)}, u32[]{:S(2)}) %copy-start) | copy-done | bytes 2097176
  1.6 0.0 copy-start.1
  1.6 0.9 %copy-done.1 = bf16[512,256]{1,0:T(8,128)(2,1)S(1)} copy-done((bf16[512,256]{1,0:T(8,128)(2,1)S(1)}, bf16[512,256]{1,0:T(8,128)(2,1)}, u32[]{:S(2)}) %copy-start.1) | copy-done | bytes 262168
  2.5 0.0 copy-start.2
  2.5 0.7 %copy-done.2 = s32[512]{0:T(512)S(1)} copy-done((s32[512]{0:T(512)S(1)}, s32[512]{0:T(512)}, u32[]{:S(2)}) %copy-start.2) | copy-done | bytes 2072
  3.2 0.0 copy-start.3
  3.2 0.7 %copy-done.3 = s32[512,1]{0,1:T(1,128)S(1)} copy-done((s32[512,1]{0,1:T(1,128)S(1)}, s32[512,1]{0,1:T(1,128)}, u32[]{:S(2)}) %copy-start.3) | copy-done | bytes 2072
  3.9 0.0 copy-start.4
  3.9 0.7 %copy-done.4 = f32[512]{0:T(512)S(1)} copy-done((f32[512]{0:T(512)S(1)}, f32[512]{0:T(512)}, u32[]{:S(2)}) %copy-start.4) | copy-done | bytes 2072
  4.6 40.0 %sums.1 = (f32[256,256]{1,0:T(8,128)S(1)}, f32[256,256]{1,0:T(8,128)S(1)}) custom-call(s32[1,512]{1,0:T(1,128)S(1)} %bitcast.3, s32[1,512]{1,0:T(1,128)S(1)} %bitcast.4, f32[1,512]{1,0:T(1,128)S(1)} %bitcast.5, bf16[4096,256]{1,0:T(8,128)(2,1)S(1)} %copy-done, bf16[512,256]{1,0:T(8,128)(2,1)S(1)} %copy-done.1), custom_call_target="tpu_custom_call" | custom-call | tf_op jit(solution)/shard_map/sums/pallas_call | solution.py:232
  44.6 13.7 %update.1 = bf16[16384,256]{1,0:T(8,128)(2,1)} custom-call(f32[256,256]{1,0:T(8,128)S(1)} %get-tuple-element.7.gram, f32[256,256]{1,0:T(8,128)S(1)} %get-tuple-element.8.cross, bf16[16384,256]{1,0:T(8,128)(2,1)} %values.1), custom_call_target="tpu_custom_call" | custom-call | tf_op jit(solution)/shard_map/update/pallas_call | solution.py:345
Async XLA Ops:
  0.0 1.6 %copy-start = (bf16[4096,256]{1,0:T(8,128)(2,1)S(1)}, bf16[4096,256]{1,0:T(8,128)(2,1)}, u32[]{:S(2)}) copy-start(bf16[4096,256]{1,0:T(8,128)(2,1)} %field.1) | copy-start | bytes 6291460
  1.6 0.9 %copy-start.1 = (bf16[512,256]{1,0:T(8,128)(2,1)S(1)}, bf16[512,256]{1,0:T(8,128)(2,1)}, u32[]{:S(2)}) copy-start(bf16[512,256]{1,0:T(8,128)(2,1)} %observed.1) | copy-start | bytes 786436
  2.5 0.7 %copy-start.2 = (s32[512]{0:T(512)S(1)}, s32[512]{0:T(512)}, u32[]{:S(2)}) copy-start(s32[512]{0:T(512)} %param.8) | copy-start | bytes 6148
  3.2 0.7 %copy-start.3 = (s32[512,1]{0,1:T(1,128)S(1)}, s32[512,1]{0,1:T(1,128)}, u32[]{:S(2)}) copy-start(s32[512,1]{0,1:T(1,128)} %param.9) | copy-start | bytes 6148
  3.9 0.7 %copy-start.4 = (f32[512]{0:T(512)S(1)}, f32[512]{0:T(512)}, u32[]{:S(2)}) copy-start(f32[512]{0:T(512)} %param.10) | copy-start | bytes 6148

commit v2 on v1

v2 whole, which is shorter than its diff:
```python
import functools
import math

import jax
import jax.numpy as jnp
from jax import lax
from jax.experimental import pallas as pl
from jax.experimental.pallas import tpu as pltpu
from jax.sharding import PartitionSpec as P

F32, BF16 = jnp.float32, jnp.bfloat16
MESH = pl.DeviceIdType.MESH
VMEM = pl.BlockSpec(memory_space=pltpu.VMEM)
HBM = pl.BlockSpec(memory_space=pltpu.HBM)
BLOCK = 512
SAFE_BOUND = 512.0
STEPS = 8
ROW_TILE = 2048


def dot(a, b):
    return lax.dot_general(a, b, (((1,), (0,)), ((), ())), preferred_element_type=F32)


def dot_rows(a, b):
    return lax.dot_general(a, b, (((0,), (0,)), ((), ())), preferred_element_type=F32)


def split(a):
    high = a.astype(BF16)
    return high, (a - high.astype(F32)).astype(BF16)


def dot_split(a, b_high, b_low):
    a_high, a_low = split(a)
    return dot(a_high, b_high) + (dot(a_low, b_high) + dot(a_high, b_low))


def exchange(
    groups,
    tiles,
    position,
    bucket,
    sigma,
    field,
    observed,
    inverse_out,
    gram_out,
    cross_out,
    bound_out,
    position_vmem,
    bucket_vmem,
    sigma_vmem,
    observed_vmem,
    field_vmem,
    picked,
    send_rows,
    got_rows,
    gram_part,
    gram_pieces,
    gram_mine,
    gram_whole,
    cross_part,
    cross_pieces,
    cross_mine,
    pair,
    small_sem,
    field_sem,
    send_sem,
    got_sem,
    piece_send,
    piece_got,
    whole_send,
    whole_got,
):
    cells, members = field.shape
    sensors = position.shape[1]
    capacity = sensors // 4
    half = members // 2
    root_scale = math.sqrt(members - 1)
    my_group, my_tile = lax.axis_index("grp"), lax.axis_index("tile")
    ys, side = groups // 2, math.isqrt(tiles)

    def other_group(offset):
        far, core = offset // 2, offset % 2
        there = lax.rem(my_group // 2 + far, ys)
        return there * 2 + lax.rem(my_group + core, 2)

    def other_tile(offset, sign=1):
        far, near = offset // side, offset % side
        far, near = (far, near) if sign > 0 else (side - far, side - near)
        z = lax.rem(my_tile // side + far, side)
        return z * side + lax.rem(lax.rem(my_tile, side) + near, side)

    def ring(step, size):
        return min(step, size - step)

    tile_order = sorted(
        range(1, tiles), key=lambda o: -ring(o // side, side) - ring(o % side, side)
    )
    group_order = sorted(range(1, groups), key=lambda o: -ring(o // 2, ys))

    small = [
        pltpu.make_async_copy(source, landing, small_sem.at[number])
        for number, (source, landing) in enumerate(
            (
                (position, position_vmem),
                (bucket, bucket_vmem),
                (sigma, sigma_vmem),
                (observed, observed_vmem),
            )
        )
    ]
    for copy in small[:3]:
        copy.start()
    loads = []
    for block in range(cells // BLOCK):
        part_rows = pl.ds(block * BLOCK, BLOCK)
        loads.append(
            pltpu.make_async_copy(field.at[part_rows], field_vmem.at[part_rows], field_sem.at[block])
        )
        loads[-1].start()
    small[3].start()

    barrier = pltpu.get_barrier_semaphore()
    for offset in group_order:
        pl.semaphore_signal(
            barrier, inc=1, device_id={"grp": other_group(offset)}, device_id_type=MESH
        )
    for offset in tile_order:
        pl.semaphore_signal(
            barrier, inc=1, device_id={"tile": other_tile(offset)}, device_id_type=MESH
        )

    for copy in small[:3]:
        copy.wait()
    cell = position_vmem[...]
    group = bucket_vmem[...]
    facts = jnp.concatenate(
        [cell.astype(F32), sigma_vmem[...], jnp.zeros((6, sensors), F32)], axis=0
    ).T
    cell_column, sigma_column = facts[:, 0:1].astype(jnp.int32), facts[:, 1:2]

    lane = lax.broadcasted_iota(jnp.int32, (sensors, sensors), 1)
    row = lax.broadcasted_iota(jnp.int32, (sensors, sensors), 0)
    earlier = (row < lane).astype(F32).astype(BF16)
    member_of = (lax.broadcasted_iota(jnp.int32, (groups, sensors), 0) == group).astype(F32)
    before = dot(member_of.astype(BF16), earlier)
    rank = jnp.sum(before * member_of, axis=0, keepdims=True).astype(jnp.int32)
    target = group * capacity + rank

    for block in range(cells // BLOCK):
        part_rows = pl.ds(block * BLOCK, BLOCK)
        chosen = (
            lax.broadcasted_iota(jnp.int32, (sensors, BLOCK), 1) == cell_column - block * BLOCK
        )
        loads[block].wait()
        value = dot(chosen.astype(F32).astype(BF16), field_vmem[part_rows, :])
        if block == 0:
            picked[...] = value
        else:
            picked[...] += value

    kept = picked[...]
    mean = jnp.mean(kept, axis=1, keepdims=True)
    scaled = ((kept - mean) / (sigma_column * root_scale)).astype(BF16)
    small[3].wait()
    misfit = ((observed_vmem[...].astype(F32) - kept) / sigma_column).astype(BF16)

    def place(values, offset):
        slot = other_group(offset) * capacity + lax.broadcasted_iota(
            jnp.int32, (capacity, sensors), 0
        )
        return dot((slot == target).astype(F32).astype(BF16), values).astype(BF16)

    def row_copy(kind, offset):
        return pltpu.make_async_remote_copy(
            src_ref=send_rows.at[kind, offset],
            dst_ref=got_rows.at[kind, offset],
            send_sem=send_sem.at[kind, offset],
            recv_sem=got_sem.at[kind, offset],
            device_id={"grp": other_group(offset)},
            device_id_type=MESH,
        )

    for kind, values in enumerate((scaled, misfit)):
        ready = None
        for offset in group_order + [0]:
            send_rows[kind, offset] = place(values, offset)
            if ready is None and kind == 0:
                pl.semaphore_wait(barrier, groups + tiles - 2)
            if ready is not None:
                row_copy(kind, ready).start()
            ready = offset

    gram = (0, gram_part, gram_pieces, gram_mine, gram_whole)
    cross = (1, cross_part, cross_pieces, cross_mine, cross_out)

    def rows_of(mine, tile):
        rows = mine.shape[0]
        return pl.ds(pl.multiple_of(tile * rows, rows), rows)

    def piece_copy(one, offset):
        which, part, pieces, mine, _ = one
        return pltpu.make_async_remote_copy(
            src_ref=part.at[rows_of(mine, other_tile(offset))],
            dst_ref=pieces.at[offset],
            send_sem=piece_send.at[which, offset],
            recv_sem=piece_got.at[which, offset],
            device_id={"tile": other_tile(offset)},
            device_id_type=MESH,
        )

    def whole_copy(one, offset, owner):
        which, _, _, mine, whole = one
        return pltpu.make_async_remote_copy(
            src_ref=mine,
            dst_ref=whole.at[rows_of(mine, owner)],
            send_sem=whole_send.at[which, offset],
            recv_sem=whole_got.at[which, offset],
            device_id={"tile": other_tile(offset)},
            device_id_type=MESH,
        )

    def add_up(kind):
        total = dot_rows(send_rows[0, 0], send_rows[kind, 0])
        for offset in group_order:
            row_copy(kind, offset).wait_recv()
            total = total + dot_rows(got_rows[0, offset], got_rows[kind, offset])
        return total

    def send_pieces(one):
        for offset in tile_order:
            piece_copy(one, offset).start()

    def spread(one):
        _, part, pieces, mine, whole = one
        total = part[rows_of(mine, my_tile)]
        for offset in tile_order[::-1]:
            piece_copy(one, offset).wait_recv()
            total = total + pieces[offset]
        mine[...] = total
        whole[rows_of(mine, my_tile)] = total
        for offset in tile_order:
            whole_copy(one, offset, my_tile).start()

    def finish(one):
        for offset in tile_order[::-1]:
            whole_copy(one, offset, other_tile(offset, -1)).wait_recv()

    total = add_up(0)
    gram_part[0:half] = total[:half, :half]
    gram_part[half : 2 * half] = total[:half, half:]
    gram_part[2 * half :] = total[half:, half:]
    send_pieces(gram)
    spread(gram)
    cross_part[...] = add_up(1)
    send_pieces(cross)

    finish(gram)
    gram_out[:half, :half] = gram_whole[0:half]
    gram_out[:half, half:] = gram_whole[half : 2 * half]
    gram_out[half:, :half] = gram_whole[half : 2 * half].T
    gram_out[half:, half:] = gram_whole[2 * half :]

    identity = (
        lax.broadcasted_iota(jnp.int32, (members, members), 0)
        == lax.broadcasted_iota(jnp.int32, (members, members), 1)
    ).astype(F32)
    matrix = gram_out[...] + identity
    bound = jnp.max(jnp.sum(jnp.abs(matrix), axis=1, keepdims=True), axis=0, keepdims=True)
    bound_out[...] = jnp.broadcast_to(bound, bound_out.shape)

    low_end, high_end = jnp.ones_like(bound), bound
    for step in range(STEPS):
        scale = 2.0 / (low_end + high_end)
        low_end = scale * low_end * (2.0 - scale * low_end)
        high_end = jnp.ones_like(bound)
        if step == 0:
            factor = 2.0 * scale * identity - (scale * scale) * matrix
            pair[:members] = factor
            high, low = split(factor)
            pair[members:] = dot_split(matrix, high, low)
        else:
            factor = 2.0 * scale * identity - (scale * scale) * pair[members:]
            high, low = split(factor)
            if step == STEPS - 1:
                inverse_out[...] = dot_split(pair[:members], high, low)
            else:
                pair[...] = dot_split(pair[...], high, low)
        if step == STEPS // 2:
            spread(cross)

    finish(cross)
    for kind in range(2):
        for offset in group_order:
            row_copy(kind, offset).wait_send()
    for one in (gram, cross):
        for offset in tile_order:
            piece_copy(one, offset).wait_send()
            whole_copy(one, offset, my_tile).wait_send()


def sums(groups, tiles, position, bucket, sigma, field, observed):
    cells, members = field.shape
    sensors = position.shape[1]
    capacity = sensors // 4
    half = members // 2
    square = jax.ShapeDtypeStruct((members, members), F32)
    inputs = (position, bucket, sigma, field, observed)
    return pl.pallas_call(
        functools.partial(exchange, groups, tiles),
        out_shape=[square, square, square, jax.ShapeDtypeStruct((8, 128), F32)],
        in_specs=[HBM] * 5,
        out_specs=[VMEM] * 4,
        scratch_shapes=[
            pltpu.VMEM((1, sensors), jnp.int32),
            pltpu.VMEM((1, sensors), jnp.int32),
            pltpu.VMEM((1, sensors), F32),
            pltpu.VMEM((sensors, members), BF16),
            pltpu.VMEM((cells, members), BF16),
            pltpu.VMEM((sensors, members), F32),
            pltpu.VMEM((2, groups, capacity, members), BF16),
            pltpu.VMEM((2, groups, capacity, members), BF16),
            pltpu.VMEM((3 * half, half), F32),
            pltpu.VMEM((tiles, 3 * half // tiles, half), F32),
            pltpu.VMEM((3 * half // tiles, half), F32),
            pltpu.VMEM((3 * half, half), F32),
            pltpu.VMEM((members, members), F32),
            pltpu.VMEM((tiles, members // tiles, members), F32),
            pltpu.VMEM((members // tiles, members), F32),
            pltpu.VMEM((2 * members, members), F32),
            pltpu.SemaphoreType.DMA((4,)),
            pltpu.SemaphoreType.DMA((cells // BLOCK,)),
            pltpu.SemaphoreType.DMA((2, groups)),
            pltpu.SemaphoreType.DMA((2, groups)),
            pltpu.SemaphoreType.DMA((2, tiles)),
            pltpu.SemaphoreType.DMA((2, tiles)),
            pltpu.SemaphoreType.DMA((2, tiles)),
            pltpu.SemaphoreType.DMA((2, tiles)),
        ],
        compiler_params=pltpu.CompilerParams(
            collective_id=0, has_side_effects=True, vmem_limit_bytes=24 << 20
        ),
        cost_estimate=pl.CostEstimate(
            flops=4 << 30, bytes_accessed=100 << 20, transcendentals=0
        ),
        name="sums",
    )(*(pltpu.with_memory_space_constraint(x, pltpu.HBM) for x in inputs))


def apply(ready, gram, cross, bound, values, out, stored, inverse, transform, store_sem):
    total_rows, members = values.shape
    steps = total_rows // ROW_TILE
    safe = bound[0, 0] <= SAFE_BOUND

    def finish(matrix):
        high, low = split(cross[...])
        weights = dot_split(matrix, high, low)
        transform[...] = (weights / math.sqrt(members - 1)).astype(BF16)

    @pl.when(safe)
    def _():
        finish(ready[...])

    @pl.when(jnp.logical_not(safe))
    def _():
        down = lax.broadcasted_iota(jnp.int32, (members, members), 0)
        along = lax.broadcasted_iota(jnp.int32, (members, members), 1)
        inverse[...] = gram[...] + (down == along).astype(F32)
        line = lax.broadcasted_iota(jnp.int32, (members, 1), 0)
        spot = lax.broadcasted_iota(jnp.int32, (1, members), 1)

        def eliminate(step, _):
            now = inverse[...]
            here, there = (line == step), (spot == step)
            row = jnp.sum(jnp.where(here, now, 0.0), axis=0, keepdims=True)
            column = jnp.sum(jnp.where(there, now, 0.0), axis=1, keepdims=True)
            pivot = jnp.sum(jnp.where(there, row, 0.0), axis=1, keepdims=True)
            row = jnp.where(there, 1.0, row) / pivot
            column = jnp.where(here, 0.0, column)
            base = jnp.where(there, 0.0, now)
            inverse[...] = jnp.where(here, row, base - column * row)
            return 0

        lax.fori_loop(0, members, eliminate, 0)
        finish(inverse[...])

    def store(step, slot):
        part = pl.ds(step * ROW_TILE, ROW_TILE)
        return pltpu.make_async_copy(stored.at[slot], out.at[part], store_sem.at[slot])

    for step in range(steps):
        slot = step % 2
        now = values[pl.ds(step * ROW_TILE, ROW_TILE), :].astype(F32)
        anomaly = (now - jnp.mean(now, axis=1, keepdims=True)).astype(BF16)
        change = dot(anomaly, transform[...])
        if step >= 2:
            store(step - 2, slot).wait()
        stored[slot] = (now + change).astype(BF16)
        store(step, slot).start()
    for step in range(steps - 2, steps):
        store(step, step % 2).wait()


def update(inverse, gram, cross, bound, values):
    total_rows, members = values.shape
    return pl.pallas_call(
        apply,
        out_shape=jax.ShapeDtypeStruct(values.shape, values.dtype),
        in_specs=[VMEM] * 5,
        out_specs=HBM,
        scratch_shapes=[
            pltpu.VMEM((2, ROW_TILE, members), BF16),
            pltpu.VMEM((members, members), F32),
            pltpu.VMEM((members, members), BF16),
            pltpu.SemaphoreType.DMA((2,)),
        ],
        compiler_params=pltpu.CompilerParams(vmem_limit_bytes=32 << 20),
        name="update",
    )(inverse, gram, cross, bound, values)


def solution(mesh):
    groups, tiles = mesh.shape["grp"], mesh.shape["tile"]

    def shards(coefficients, field, position, bucket, sigma, observed):
        sensors = position.shape[0]
        solved = sums(
            groups,
            tiles,
            position.reshape(1, sensors),
            bucket.reshape(1, sensors),
            sigma.reshape(1, sensors),
            field,
            observed,
        )
        return update(*solved, coefficients)

    rows, flat = P(("grp", "tile"), None), P(("grp", "tile"))
    return jax.shard_map(
        shards,
        mesh=mesh,
        in_specs=(rows, rows, flat, rows, flat, rows),
        out_specs=rows,
        check_vma=False,
    )
```

time: 58.6 us -> 50.4 us (0.86)
  local copies, waits for them, and re-layouts: 4.58 us -> 0.01 us
  Pallas kernels: 53.6 us -> 50.1 us
    pallas_call x1, Pallas kernels: 13.7 us -> 8.5 us  [update(): pl.pallas_call(apply, out_shape=jax.ShapeDtypeStruct(values.shape, values...]
    unnamed x10 -> x4, local copies, waits for them, and re-layouts: 4.58 us -> 0.01 us
    pallas_call x1, Pallas kernels: 40 us -> 41.7 us  [sums(): pl.pallas_call(functools.partial(exchange, groups, tiles), out_shape=[squ...]
where the time goes in v2:
time: 50.4 us; the launch traced here: 50.3 us
  Pallas kernels  50.1 us (99%)
    pallas_call x1, Pallas kernels, sums(): pl.pallas_call(functools.partial(exchange, groups, tiles), out_shape=[squ...  41.7 us
    pallas_call x1, Pallas kernels, update(): pl.pallas_call(apply, out_shape=jax.ShapeDtypeStruct(values.shape, values...  8.5 us

profile of v2, /device:TPU:0, one launch (start us, length us, event | category | flops | bytes accessed | tf_op | source)
XLA Modules:
  0.0 50.3 jit_solution(914531291413004112)
XLA Ops:
  0.0 0.0 slice-start
  0.0 0.0 slice-start.1
  0.0 41.7 %sums.1 = (f32[256,256]{1,0:T(8,128)S(1)}, f32[256,256]{1,0:T(8,128)S(1)}, f32[256,256]{1,0:T(8,128)S(1)}, f32[8,128]{1,0:T(8,128)S(1)}) custom-call(s32[1,512]{1,0:T(1,128)} %bitcast.5, s32[1,512]{1,0:T(1,128)} %bitcast.6, f32[1,512]{1,0:T(1,128)} %bitcast.7, bf16[4096,256]{1,0:T(8,128)(2,1)} %field.1, bf16[512,256]{1,0:T(8,128)(2,1)} %observed.1), custom_call_target="tpu_custom_call" | custom-call | flops 4294967296 | bytes 104857600 | tf_op jit(solution)/shard_map/sums/pallas_call | solution.py:311
  41.7 0.0 slice-done
  41.7 0.0 slice-done.1
  41.7 8.5 %update.1 = bf16[16384,256]{1,0:T(8,128)(2,1)} custom-call(f32[256,256]{1,0:T(8,128)S(1)} %get-tuple-element.9.ready, f32[256,256]{1,0:T(8,128)S(1)} %get-tuple-element.10.gram, f32[256,256]{1,0:T(8,128)S(1)} %get-tuple-element.11.cross, f32[8,128]{1,0:T(8,128)S(1)} %get-tuple-element.12.bound, bf16[16384,256]{1,0:T(8,128)(2,1)S(1)} %bitcast.4), custom_call_target="tpu_custom_call" | custom-call | tf_op jit(solution)/shard_map/update/pallas_call | solution.py:408
  (1 shorter events, 0.0 us)
Async XLA Ops:
  0.0 41.7 %slice-start = ((s8[8388608]{0:T(1024)(128)(4,1)}), s8[4194304]{0:T(1024)(128)(4,1)S(1)}, s32[]{:S(2)}) async-start(s8[8388608]{0:T(1024)(128)(4,1)} %bitcast.3), calls=%async_computation | async-start | bytes 8388608
  0.0 41.7 %slice-start.1 = ((s8[8388608]{0:T(1024)(128)(4,1)}), s8[4194304]{0:T(1024)(128)(4,1)S(1)}, s32[]{:S(2)}) async-start(s8[8388608]{0:T(1024)(128)(4,1)} %bitcast.3), calls=%async_computation.1 | async-start | bytes 8388608

commit v3 on v2

--- a/solution.py
+++ b/solution.py
@@ -16,6 +16,7 @@
 SAFE_BOUND = 512.0
 STEPS = 8
 ROW_TILE = 2048
+STORE_TILE = 1024
 
 
 def dot(a, b):
@@ -44,10 +45,13 @@
     sigma,
     field,
     observed,
+    coefficients,
     inverse_out,
     gram_out,
     cross_out,
     bound_out,
+    values_out,
+    anomaly_out,
     position_vmem,
     bucket_vmem,
     sigma_vmem,
@@ -66,6 +70,7 @@
     pair,
     small_sem,
     field_sem,
+    value_sem,
     send_sem,
     got_sem,
     piece_send,
@@ -122,6 +127,14 @@
         loads[-1].start()
     small[3].start()
 
+    def value_load(step):
+        part_rows = pl.ds(pl.multiple_of(step * ROW_TILE, ROW_TILE), ROW_TILE)
+        return pltpu.make_async_copy(
+            coefficients.at[part_rows], values_out.at[part_rows], value_sem.at[step]
+        )
+
+    value_steps = coefficients.shape[0] // ROW_TILE
+
     barrier = pltpu.get_barrier_semaphore()
     for offset in group_order:
         pl.semaphore_signal(
@@ -192,6 +205,17 @@
             if ready is not None:
                 row_copy(kind, ready).start()
             ready = offset
+
+    def center(step, _):
+        value_load(step).wait()
+        part_rows = pl.ds(pl.multiple_of(step * ROW_TILE, ROW_TILE), ROW_TILE)
+        now = values_out[part_rows, :].astype(F32)
+        anomaly_out[part_rows, :] = (now - jnp.mean(now, axis=1, keepdims=True)).astype(BF16)
+        return 0
+
+    for step in range(value_steps):
+        value_load(step).start()
+    lax.fori_loop(0, value_steps, center, 0)
 
     gram = (0, gram_part, gram_pieces, gram_mine, gram_whole)
     cross = (1, cross_part, cross_pieces, cross_mine, cross_out)
@@ -301,18 +325,20 @@
             whole_copy(one, offset, my_tile).wait_send()
 
 
-def sums(groups, tiles, position, bucket, sigma, field, observed):
+def sums(groups, tiles, position, bucket, sigma, field, observed, coefficients):
     cells, members = field.shape
     sensors = position.shape[1]
     capacity = sensors // 4
     half = members // 2
     square = jax.ShapeDtypeStruct((members, members), F32)
-    inputs = (position, bucket, sigma, field, observed)
+    ensemble = jax.ShapeDtypeStruct(coefficients.shape, coefficients.dtype)
+    inputs = (position, bucket, sigma, field, observed, coefficients)
     return pl.pallas_call(
         functools.partial(exchange, groups, tiles),
-        out_shape=[square, square, square, jax.ShapeDtypeStruct((8, 128), F32)],
-        in_specs=[HBM] * 5,
-        out_specs=[VMEM] * 4,
+        out_shape=[square, square, square, jax.ShapeDtypeStruct((8, 128), F32)]
+        + [ensemble] * 2,
+        in_specs=[HBM] * 6,
+        out_specs=[VMEM] * 6,
         scratch_shapes=[
             pltpu.VMEM((1, sensors), jnp.int32),
             pltpu.VMEM((1, sensors), jnp.int32),
@@ -332,6 +358,7 @@
             pltpu.VMEM((2 * members, members), F32),
             pltpu.SemaphoreType.DMA((4,)),
             pltpu.SemaphoreType.DMA((cells // BLOCK,)),
+            pltpu.SemaphoreType.DMA((coefficients.shape[0] // ROW_TILE,)),
             pltpu.SemaphoreType.DMA((2, groups)),
             pltpu.SemaphoreType.DMA((2, groups)),
             pltpu.SemaphoreType.DMA((2, tiles)),
@@ -340,7 +367,7 @@
             pltpu.SemaphoreType.DMA((2, tiles)),
         ],
         compiler_params=pltpu.CompilerParams(
-            collective_id=0, has_side_effects=True, vmem_limit_bytes=24 << 20
+            collective_id=0, has_side_effects=True, vmem_limit_bytes=16 << 20
         ),
         cost_estimate=pl.CostEstimate(
             flops=4 << 30, bytes_accessed=100 << 20, transcendentals=0
@@ -349,9 +376,9 @@
     )(*(pltpu.with_memory_space_constraint(x, pltpu.HBM) for x in inputs))
 
 
-def apply(ready, gram, cross, bound, values, out, stored, inverse, transform, store_sem):
+def apply(ready, gram, cross, bound, values, anomaly, out, stored, inverse, transform, store_sem):
     total_rows, members = values.shape
-    steps = total_rows // ROW_TILE
+    steps = total_rows // STORE_TILE
     safe = bound[0, 0] <= SAFE_BOUND
 
     def finish(matrix):
@@ -386,39 +413,35 @@
         lax.fori_loop(0, members, eliminate, 0)
         finish(inverse[...])
 
-    def store(step, slot):
-        part = pl.ds(step * ROW_TILE, ROW_TILE)
-        return pltpu.make_async_copy(stored.at[slot], out.at[part], store_sem.at[slot])
+    def store(step):
+        rows = pl.ds(step * STORE_TILE, STORE_TILE)
+        return pltpu.make_async_copy(stored.at[rows], out.at[rows], store_sem.at[step])
 
     for step in range(steps):
-        slot = step % 2
-        now = values[pl.ds(step * ROW_TILE, ROW_TILE), :].astype(F32)
-        anomaly = (now - jnp.mean(now, axis=1, keepdims=True)).astype(BF16)
-        change = dot(anomaly, transform[...])
-        if step >= 2:
-            store(step - 2, slot).wait()
-        stored[slot] = (now + change).astype(BF16)
-        store(step, slot).start()
-    for step in range(steps - 2, steps):
-        store(step, step % 2).wait()
-
-
-def update(inverse, gram, cross, bound, values):
+        rows = pl.ds(step * STORE_TILE, STORE_TILE)
+        change = dot(anomaly[rows, :], transform[...])
+        stored[rows, :] = (values[rows, :].astype(F32) + change).astype(BF16)
+        store(step).start()
+    for step in range(steps):
+        store(step).wait()
+
+
+def update(inverse, gram, cross, bound, values, anomaly):
     total_rows, members = values.shape
     return pl.pallas_call(
         apply,
         out_shape=jax.ShapeDtypeStruct(values.shape, values.dtype),
-        in_specs=[VMEM] * 5,
+        in_specs=[VMEM] * 6,
         out_specs=HBM,
         scratch_shapes=[
-            pltpu.VMEM((2, ROW_TILE, members), BF16),
+            pltpu.VMEM((total_rows, members), BF16),
             pltpu.VMEM((members, members), F32),
             pltpu.VMEM((members, members), BF16),
-            pltpu.SemaphoreType.DMA((2,)),
+            pltpu.SemaphoreType.DMA((total_rows // STORE_TILE,)),
         ],
-        compiler_params=pltpu.CompilerParams(vmem_limit_bytes=32 << 20),
+        compiler_params=pltpu.CompilerParams(vmem_limit_bytes=16 << 20),
         name="update",
-    )(inverse, gram, cross, bound, values)
+    )(inverse, gram, cross, bound, values, anomaly)
 
 
 def solution(mesh):
@@ -434,8 +457,9 @@
             sigma.reshape(1, sensors),
             field,
             observed,
-        )
-        return update(*solved, coefficients)
+            coefficients,
+        )
+        return update(*solved)
 
     rows, flat = P(("grp", "tile"), None), P(("grp", "tile"))
     return jax.shard_map(

time: 50.4 us -> 46 us (0.913)
  Pallas kernels: 50.1 us -> 45.8 us
    pallas_call x1, Pallas kernels: 8.5 us -> 4.27 us  [update(): pl.pallas_call(apply, out_shape=jax.ShapeDtypeStruct(values.shape, values...]
where the time goes in v3:
time: 46 us; the launch traced here: 45.8 us
  Pallas kernels  45.8 us (100%)
    pallas_call x1, Pallas kernels, sums(): pl.pallas_call(functools.partial(exchange, groups, tiles), out_shape=[squ...  41.6 us
    pallas_call x1, Pallas kernels, update(): pl.pallas_call(apply, out_shape=jax.ShapeDtypeStruct(values.shape, values...  4.27 us

profile of v3, /device:TPU:0, one launch (start us, length us, event | category | flops | bytes accessed | tf_op | source)
XLA Modules:
  0.0 45.8 jit_solution(18114563645339102859)
XLA Ops:
  0.0 41.6 %sums.1 = (f32[256,256]{1,0:T(8,128)S(1)}, f32[256,256]{1,0:T(8,128)S(1)}, f32[256,256]{1,0:T(8,128)S(1)}, f32[8,128]{1,0:T(8,128)S(1)}, bf16[16384,256]{1,0:T(8,128)(2,1)S(1)}, /*index=5*/bf16[16384,256]{1,0:T(8,128)(2,1)S(1)}) custom-call(s32[1,512]{1,0:T(1,128)} %bitcast.3, s32[1,512]{1,0:T(1,128)} %bitcast.4, f32[1,512]{1,0:T(1,128)} %bitcast.5, ...), custom_call_target="tpu_custom_call" | custom-call | flops 4294967296 | bytes 104857600 | tf_op jit(solution)/shard_map/sums/pallas_call | solution.py:336
  41.6 4.3 %update.1 = bf16[16384,256]{1,0:T(8,128)(2,1)} custom-call(f32[256,256]{1,0:T(8,128)S(1)} %get-tuple-element.11.ready, f32[256,256]{1,0:T(8,128)S(1)} %get-tuple-element.12.gram, f32[256,256]{1,0:T(8,128)S(1)} %get-tuple-element.13.cross, f32[8,128]{1,0:T(8,128)S(1)} %get-tuple-element.14.bound, bf16[16384,256]{1,0:T(8,128)(2,1)S(1)} %get-tuple-element.15.values, ...), custom_call_target="tpu_custom_call" | custom-call | tf_op jit(solution)/shard_map/update/pallas_call | solution.py:431

commit v4 on v3

--- a/solution.py
+++ b/solution.py
@@ -12,7 +12,8 @@
 MESH = pl.DeviceIdType.MESH
 VMEM = pl.BlockSpec(memory_space=pltpu.VMEM)
 HBM = pl.BlockSpec(memory_space=pltpu.HBM)
-BLOCK = 512
+BLOCK = 2048
+LANES = 128
 SAFE_BOUND = 512.0
 STEPS = 8
 ROW_TILE = 2048
@@ -60,6 +61,8 @@
     picked,
     send_rows,
     got_rows,
+    send_half,
+    got_half,
     gram_part,
     gram_pieces,
     gram_mine,
@@ -67,6 +70,7 @@
     cross_part,
     cross_pieces,
     cross_mine,
+    cross_whole,
     pair,
     small_sem,
     field_sem,
@@ -145,66 +149,94 @@
             barrier, inc=1, device_id={"tile": other_tile(offset)}, device_id_type=MESH
         )
 
-    for copy in small[:3]:
-        copy.wait()
-    cell = position_vmem[...]
-    group = bucket_vmem[...]
-    facts = jnp.concatenate(
-        [cell.astype(F32), sigma_vmem[...], jnp.zeros((6, sensors), F32)], axis=0
-    ).T
-    cell_column, sigma_column = facts[:, 0:1].astype(jnp.int32), facts[:, 1:2]
-
     lane = lax.broadcasted_iota(jnp.int32, (sensors, sensors), 1)
     row = lax.broadcasted_iota(jnp.int32, (sensors, sensors), 0)
     earlier = (row < lane).astype(F32).astype(BF16)
+    for copy in small[:3]:
+        copy.wait()
+    cell = position_vmem[...].astype(F32)
+    block_of = jnp.floor(cell * (1.0 / LANES))
+    inverse_sigma = 1.0 / sigma_vmem[...]
+    facts = jnp.concatenate(
+        [
+            block_of,
+            cell - block_of * LANES,
+            inverse_sigma,
+            inverse_sigma * (1.0 / root_scale),
+            jnp.zeros((4, sensors), F32),
+        ],
+        axis=0,
+    ).T
+    block_column = jnp.broadcast_to(facts[:, 0:1], (sensors, LANES)).astype(BF16)
+    spots = lax.broadcasted_iota(jnp.int32, (sensors, LANES), 1).astype(F32)
+    spot_hit = (spots == facts[:, 1:2]).astype(F32).astype(BF16)
+    none = jnp.zeros_like(spot_hit)
+
+    value = None
+    for block in range(cells // BLOCK):
+        chosen = jnp.concatenate(
+            [
+                jnp.where(block_column == float(block * (BLOCK // LANES) + k), spot_hit, none)
+                for k in range(BLOCK // LANES)
+            ],
+            axis=1,
+        )
+        loads[block].wait()
+        more = dot(chosen, field_vmem[pl.ds(block * BLOCK, BLOCK), :])
+        value = more if value is None else value + more
+    picked[...] = value
+
+    group = bucket_vmem[...]
     member_of = (lax.broadcasted_iota(jnp.int32, (groups, sensors), 0) == group).astype(F32)
     before = dot(member_of.astype(BF16), earlier)
-    rank = jnp.sum(before * member_of, axis=0, keepdims=True).astype(jnp.int32)
-    target = group * capacity + rank
-
-    for block in range(cells // BLOCK):
-        part_rows = pl.ds(block * BLOCK, BLOCK)
-        chosen = (
-            lax.broadcasted_iota(jnp.int32, (sensors, BLOCK), 1) == cell_column - block * BLOCK
-        )
-        loads[block].wait()
-        value = dot(chosen.astype(F32).astype(BF16), field_vmem[part_rows, :])
-        if block == 0:
-            picked[...] = value
-        else:
-            picked[...] += value
+    rank = jnp.sum(before * member_of, axis=0, keepdims=True)
+    target = group.astype(F32) * capacity + rank
 
     kept = picked[...]
     mean = jnp.mean(kept, axis=1, keepdims=True)
-    scaled = ((kept - mean) / (sigma_column * root_scale)).astype(BF16)
+    scaled = ((kept - mean) * facts[:, 3:4]).astype(BF16)
     small[3].wait()
-    misfit = ((observed_vmem[...].astype(F32) - kept) / sigma_column).astype(BF16)
+    misfit = ((observed_vmem[...].astype(F32) - kept) * facts[:, 2:3]).astype(BF16)
+
+    slots = lax.broadcasted_iota(jnp.int32, (capacity, sensors), 0).astype(F32).astype(BF16)
 
     def place(values, offset):
-        slot = other_group(offset) * capacity + lax.broadcasted_iota(
-            jnp.int32, (capacity, sensors), 0
-        )
-        return dot((slot == target).astype(F32).astype(BF16), values).astype(BF16)
+        first = (other_group(offset) * capacity).astype(F32)
+        local = jnp.clip(target - first, -1.0, float(capacity)).astype(BF16)
+        hit = jnp.where(slots == local, jnp.ones_like(slots), jnp.zeros_like(slots))
+        return dot(hit, values).astype(BF16)
 
     def row_copy(kind, offset):
+        source, landing = send_rows.at[offset], got_rows.at[offset]
+        if kind:
+            source, landing = send_half.at[kind - 1, offset], got_half.at[kind - 1, offset]
         return pltpu.make_async_remote_copy(
-            src_ref=send_rows.at[kind, offset],
-            dst_ref=got_rows.at[kind, offset],
+            src_ref=source,
+            dst_ref=landing,
             send_sem=send_sem.at[kind, offset],
             recv_sem=got_sem.at[kind, offset],
             device_id={"grp": other_group(offset)},
             device_id_type=MESH,
         )
 
-    for kind, values in enumerate((scaled, misfit)):
-        ready = None
-        for offset in group_order + [0]:
-            send_rows[kind, offset] = place(values, offset)
-            if ready is None and kind == 0:
-                pl.semaphore_wait(barrier, groups + tiles - 2)
-            if ready is not None:
-                row_copy(kind, ready).start()
-            ready = offset
+    ready = None
+    for offset in group_order + [0]:
+        send_rows[offset] = place(scaled, offset)
+        if ready is None:
+            pl.semaphore_wait(barrier, groups + tiles - 2)
+        else:
+            row_copy(0, ready).start()
+        ready = offset
+    ready = None
+    for offset in group_order + [0]:
+        placed = place(misfit, offset)
+        send_half[0, offset] = placed[:, :half]
+        send_half[1, offset] = placed[:, half:]
+        if ready is not None:
+            row_copy(1, ready).start()
+        ready = offset
+    for offset in group_order:
+        row_copy(2, offset).start()
 
     def center(step, _):
         value_load(step).wait()
@@ -218,7 +250,16 @@
     lax.fori_loop(0, value_steps, center, 0)
 
     gram = (0, gram_part, gram_pieces, gram_mine, gram_whole)
-    cross = (1, cross_part, cross_pieces, cross_mine, cross_out)
+    crosses = [
+        (
+            1 + side_half,
+            cross_part.at[side_half],
+            cross_pieces.at[side_half],
+            cross_mine.at[side_half],
+            cross_whole.at[side_half],
+        )
+        for side_half in range(2)
+    ]
 
     def rows_of(mine, tile):
         rows = mine.shape[0]
@@ -247,10 +288,12 @@
         )
 
     def add_up(kind):
-        total = dot_rows(send_rows[0, 0], send_rows[kind, 0])
+        other = send_half.at[kind - 1] if kind else send_rows
+        total = dot_rows(send_rows[0], other[0])
+        other = got_half.at[kind - 1] if kind else got_rows
         for offset in group_order:
             row_copy(kind, offset).wait_recv()
-            total = total + dot_rows(got_rows[0, offset], got_rows[kind, offset])
+            total = total + dot_rows(got_rows[offset], other[offset])
         return total
 
     def send_pieces(one):
@@ -277,11 +320,15 @@
     gram_part[half : 2 * half] = total[:half, half:]
     gram_part[2 * half :] = total[half:, half:]
     send_pieces(gram)
+    cross_part[0] = add_up(1)
+    send_pieces(crosses[0])
     spread(gram)
-    cross_part[...] = add_up(1)
-    send_pieces(cross)
+    cross_part[1] = add_up(2)
+    send_pieces(crosses[1])
+    spread(crosses[0])
 
     finish(gram)
+    spread(crosses[1])
     gram_out[:half, :half] = gram_whole[0:half]
     gram_out[:half, half:] = gram_whole[half : 2 * half]
     gram_out[half:, :half] = gram_whole[half : 2 * half].T
@@ -312,14 +359,14 @@
                 inverse_out[...] = dot_split(pair[:members], high, low)
             else:
                 pair[...] = dot_split(pair[...], high, low)
-        if step == STEPS // 2:
-            spread(cross)
-
-    finish(cross)
-    for kind in range(2):
+
+    for side_half, one in enumerate(crosses):
+        finish(one)
+        cross_out[:, side_half * half : (side_half + 1) * half] = cross_whole[side_half]
+    for kind in range(3):
         for offset in group_order:
             row_copy(kind, offset).wait_send()
-    for one in (gram, cross):
+    for one in [gram] + crosses:
         for offset in tile_order:
             piece_copy(one, offset).wait_send()
             whole_copy(one, offset, my_tile).wait_send()
@@ -346,25 +393,28 @@
             pltpu.VMEM((sensors, members), BF16),
             pltpu.VMEM((cells, members), BF16),
             pltpu.VMEM((sensors, members), F32),
-            pltpu.VMEM((2, groups, capacity, members), BF16),
-            pltpu.VMEM((2, groups, capacity, members), BF16),
+            pltpu.VMEM((groups, capacity, members), BF16),
+            pltpu.VMEM((groups, capacity, members), BF16),
+            pltpu.VMEM((2, groups, capacity, half), BF16),
+            pltpu.VMEM((2, groups, capacity, half), BF16),
             pltpu.VMEM((3 * half, half), F32),
             pltpu.VMEM((tiles, 3 * half // tiles, half), F32),
             pltpu.VMEM((3 * half // tiles, half), F32),
             pltpu.VMEM((3 * half, half), F32),
-            pltpu.VMEM((members, members), F32),
-            pltpu.VMEM((tiles, members // tiles, members), F32),
-            pltpu.VMEM((members // tiles, members), F32),
+            pltpu.VMEM((2, members, half), F32),
+            pltpu.VMEM((2, tiles, members // tiles, half), F32),
+            pltpu.VMEM((2, members // tiles, half), F32),
+            pltpu.VMEM((2, members, half), F32),
             pltpu.VMEM((2 * members, members), F32),
             pltpu.SemaphoreType.DMA((4,)),
             pltpu.SemaphoreType.DMA((cells // BLOCK,)),
             pltpu.SemaphoreType.DMA((coefficients.shape[0] // ROW_TILE,)),
-            pltpu.SemaphoreType.DMA((2, groups)),
-            pltpu.SemaphoreType.DMA((2, groups)),
-            pltpu.SemaphoreType.DMA((2, tiles)),
-            pltpu.SemaphoreType.DMA((2, tiles)),
-            pltpu.SemaphoreType.DMA((2, tiles)),
-            pltpu.SemaphoreType.DMA((2, tiles)),
+            pltpu.SemaphoreType.DMA((3, groups)),
+            pltpu.SemaphoreType.DMA((3, groups)),
+            pltpu.SemaphoreType.DMA((3, tiles)),
+            pltpu.SemaphoreType.DMA((3, tiles)),
+            pltpu.SemaphoreType.DMA((3, tiles)),
+            pltpu.SemaphoreType.DMA((3, tiles)),
         ],
         compiler_params=pltpu.CompilerParams(
             collective_id=0, has_side_effects=True, vmem_limit_bytes=16 << 20

time: 46 us -> 42.2 us (0.917)
  Pallas kernels: 45.8 us -> 42.1 us
    pallas_call x1, Pallas kernels: 41.6 us -> 37.8 us  [sums(): pl.pallas_call(functools.partial(exchange, groups, tiles), out_shape=[squ...]
where the time goes in v4:
time: 42.2 us; the launch traced here: 42.1 us
  Pallas kernels  42.1 us (100%)
    pallas_call x1, Pallas kernels, sums(): pl.pallas_call(functools.partial(exchange, groups, tiles), out_shape=[squ...  37.8 us
    pallas_call x1, Pallas kernels, update(): pl.pallas_call(apply, out_shape=jax.ShapeDtypeStruct(values.shape, values...  4.27 us

profile of v4, /device:TPU:0, one launch (start us, length us, event | category | flops | bytes accessed | tf_op | source)
XLA Modules:
  0.0 42.1 jit_solution(17352709608782048449)
XLA Ops:
  0.0 37.8 %sums.1 = (f32[256,256]{1,0:T(8,128)S(1)}, f32[256,256]{1,0:T(8,128)S(1)}, f32[256,256]{1,0:T(8,128)S(1)}, f32[8,128]{1,0:T(8,128)S(1)}, bf16[16384,256]{1,0:T(8,128)(2,1)S(1)}, /*index=5*/bf16[16384,256]{1,0:T(8,128)(2,1)S(1)}) custom-call(s32[1,512]{1,0:T(1,128)} %bitcast.3, s32[1,512]{1,0:T(1,128)} %bitcast.4, f32[1,512]{1,0:T(1,128)} %bitcast.5, ...), custom_call_target="tpu_custom_call" | custom-call | flops 4294967296 | bytes 104857600 | tf_op jit(solution)/shard_map/sums/pallas_call | solution.py:383
  37.8 4.3 %update.1 = bf16[16384,256]{1,0:T(8,128)(2,1)} custom-call(f32[256,256]{1,0:T(8,128)S(1)} %get-tuple-element.11.ready, f32[256,256]{1,0:T(8,128)S(1)} %get-tuple-element.12.gram, f32[256,256]{1,0:T(8,128)S(1)} %get-tuple-element.13.cross, f32[8,128]{1,0:T(8,128)S(1)} %get-tuple-element.14.bound, bf16[16384,256]{1,0:T(8,128)(2,1)S(1)} %get-tuple-element.15.values, ...), custom_call_target="tpu_custom_call" | custom-call | tf_op jit(solution)/shard_map/update/pallas_call | solution.py:481

commit v5 on v4

--- a/solution.py
+++ b/solution.py
@@ -14,8 +14,8 @@
 HBM = pl.BlockSpec(memory_space=pltpu.HBM)
 BLOCK = 2048
 LANES = 128
-SAFE_BOUND = 512.0
-STEPS = 8
+SAFE_BOUND = 256.0
+STEPS = 7
 ROW_TILE = 2048
 STORE_TILE = 1024
 
@@ -322,13 +322,13 @@
     send_pieces(gram)
     cross_part[0] = add_up(1)
     send_pieces(crosses[0])
-    spread(gram)
     cross_part[1] = add_up(2)
     send_pieces(crosses[1])
+    spread(gram)
     spread(crosses[0])
 
+    spread(crosses[1])
     finish(gram)
-    spread(crosses[1])
     gram_out[:half, :half] = gram_whole[0:half]
     gram_out[:half, half:] = gram_whole[half : 2 * half]
     gram_out[half:, :half] = gram_whole[half : 2 * half].T

time: 42.2 us -> 40.9 us (0.969)
  Pallas kernels: 42.1 us -> 40.7 us
    pallas_call x1, Pallas kernels: 37.8 us -> 36.5 us  [sums(): pl.pallas_call(functools.partial(exchange, groups, tiles), out_shape=[squ...]
where the time goes in v5:
time: 40.9 us; the launch traced here: 40.8 us
  Pallas kernels  40.7 us (100%)
    pallas_call x1, Pallas kernels, sums(): pl.pallas_call(functools.partial(exchange, groups, tiles), out_shape=[squ...  36.5 us
    pallas_call x1, Pallas kernels, update(): pl.pallas_call(apply, out_shape=jax.ShapeDtypeStruct(values.shape, values...  4.26 us

profile of v5, /device:TPU:0, one launch (start us, length us, event | category | flops | bytes accessed | tf_op | source)
XLA Modules:
  0.0 40.8 jit_solution(14628273502536438110)
XLA Ops:
  0.0 36.5 %sums.1 = (f32[256,256]{1,0:T(8,128)S(1)}, f32[256,256]{1,0:T(8,128)S(1)}, f32[256,256]{1,0:T(8,128)S(1)}, f32[8,128]{1,0:T(8,128)S(1)}, bf16[16384,256]{1,0:T(8,128)(2,1)S(1)}, /*index=5*/bf16[16384,256]{1,0:T(8,128)(2,1)S(1)}) custom-call(s32[1,512]{1,0:T(1,128)} %bitcast.3, s32[1,512]{1,0:T(1,128)} %bitcast.4, f32[1,512]{1,0:T(1,128)} %bitcast.5, ...), custom_call_target="tpu_custom_call" | custom-call | flops 4294967296 | bytes 104857600 | tf_op jit(solution)/shard_map/sums/pallas_call | solution.py:383
  36.5 4.3 %update.1 = bf16[16384,256]{1,0:T(8,128)(2,1)} custom-call(f32[256,256]{1,0:T(8,128)S(1)} %get-tuple-element.11.ready, f32[256,256]{1,0:T(8,128)S(1)} %get-tuple-element.12.gram, f32[256,256]{1,0:T(8,128)S(1)} %get-tuple-element.13.cross, f32[8,128]{1,0:T(8,128)S(1)} %get-tuple-element.14.bound, bf16[16384,256]{1,0:T(8,128)(2,1)S(1)} %get-tuple-element.15.values, ...), custom_call_target="tpu_custom_call" | custom-call | tf_op jit(solution)/shard_map/update/pallas_call | solution.py:481

commit v6 on v5

--- a/solution.py
+++ b/solution.py
@@ -431,14 +431,13 @@
     steps = total_rows // STORE_TILE
     safe = bound[0, 0] <= SAFE_BOUND
 
-    def finish(matrix):
-        high, low = split(cross[...])
-        weights = dot_split(matrix, high, low)
+    def finish(weights):
         transform[...] = (weights / math.sqrt(members - 1)).astype(BF16)
 
     @pl.when(safe)
     def _():
-        finish(ready[...])
+        high, low = split(cross[...])
+        finish(dot_split(ready[...], high, low))
 
     @pl.when(jnp.logical_not(safe))
     def _():
@@ -461,7 +460,14 @@
             return 0
 
         lax.fori_loop(0, members, eliminate, 0)
-        finish(inverse[...])
+        finish(
+            jnp.dot(
+                inverse[...],
+                cross[...],
+                precision=lax.Precision.HIGHEST,
+                preferred_element_type=F32,
+            )
+        )
 
     def store(step):
         rows = pl.ds(step * STORE_TILE, STORE_TILE)

time: 40.9 us -> 40.9 us (level)
  no operation moved by 1% of the time
where the time goes in v6:
time: 40.9 us; the launch traced here: 40.8 us
  Pallas kernels  40.7 us (100%)
    pallas_call x1, Pallas kernels, sums(): pl.pallas_call(functools.partial(exchange, groups, tiles), out_shape=[squ...  36.5 us
    pallas_call x1, Pallas kernels, update(): pl.pallas_call(apply, out_shape=jax.ShapeDtypeStruct(values.shape, values...  4.26 us

profile of v6, /device:TPU:0, one launch (start us, length us, event | category | flops | bytes accessed | tf_op | source)
XLA Modules:
  0.0 40.8 jit_solution(14171545009748349508)
XLA Ops:
  0.0 36.5 %sums.1 = (f32[256,256]{1,0:T(8,128)S(1)}, f32[256,256]{1,0:T(8,128)S(1)}, f32[256,256]{1,0:T(8,128)S(1)}, f32[8,128]{1,0:T(8,128)S(1)}, bf16[16384,256]{1,0:T(8,128)(2,1)S(1)}, /*index=5*/bf16[16384,256]{1,0:T(8,128)(2,1)S(1)}) custom-call(s32[1,512]{1,0:T(1,128)} %bitcast.3, s32[1,512]{1,0:T(1,128)} %bitcast.4, f32[1,512]{1,0:T(1,128)} %bitcast.5, ...), custom_call_target="tpu_custom_call" | custom-call | flops 4294967296 | bytes 104857600 | tf_op jit(solution)/shard_map/sums/pallas_call | solution.py:383
  36.5 4.3 %update.1 = bf16[16384,256]{1,0:T(8,128)(2,1)} custom-call(f32[256,256]{1,0:T(8,128)S(1)} %get-tuple-element.11.ready, f32[256,256]{1,0:T(8,128)S(1)} %get-tuple-element.12.gram, f32[256,256]{1,0:T(8,128)S(1)} %get-tuple-element.13.cross, f32[8,128]{1,0:T(8,128)S(1)} %get-tuple-element.14.bound, bf16[16384,256]{1,0:T(8,128)(2,1)S(1)} %get-tuple-element.15.values, ...), custom_call_target="tpu_custom_call" | custom-call | tf_op jit(solution)/shard_map/update/pallas_call | solution.py:487
